TPU v7x, 32 devices: a whole 2x2x4 slice. The times are simulated.
32 devices in a mesh: row: 8 (over z, x), col: 4 (over y, core).
Axes of the slice: x: 2, y: 2, z: 4, core: 2. Of those that a mesh axis runs over, the one named last changes fastest.
Arguments:
- charges: float32 [32768], P(('row', 'col')), may hold values from -0.5 to 1.5
- structure_id: int32 [32768], P(('row', 'col')), may hold values from 0 to 255, as said below
- live_count: int32 [32], P(('row', 'col')), may hold values from 512 to 1024, as said below
- cell_index: int32 [3, 32768], P(None, ('row', 'col')), may hold values from 0 to 255, as said below
- fraction: float32 [3, 32768], P(None, ('row', 'col')), may hold values from 0 to 1
- influence: float32 [256, 64, 64], P('col', 'row'), may hold values from 0.1 to 10
Outputs:
- forces: float32 [3, 32768], P(None, ('row', 'col'))
- atom_energy: float32 [32768], P(('row', 'col'))
Inputs may be any that keep to these rules, and one draw needn't show every extreme that they name: `structure_id`: devices are numbered row-major over (row, col). Slots 0 to 7 of device d are live and belong to fragments d * 8 to d * 8 + 7, so every fragment has a live atom; every other slot names a fragment of its own device, of one of the four devices beside it along row or col (wrapping around), or of the device whose number is d plus half the number of devices (wrapping around). Device d's live atoms are its first live_count[d] slots; the count reaches 1024 on some device in every draw. `cell_index`: the atom slots of the device at (row r, col c) lie in its mesh block: first index from r * 8 to r * 8 + 7, second from c * 16 to c * 16 + 15; the third is anywhere.
All inputs are finite; a program needn't handle non-finite values.
Results may differ from a plain program's by a relative error of at most 0.000065.
Values sent between devices are 32-bit elements; how exact they have to be, the bound alone decides.
A program may use at most 64 MiB of HBM per device.

v0:
```python
import math
import jax
import jax.numpy as jnp
from jax import lax
from jax.sharding import PartitionSpec as P

CX = 8
CY = 16
NZ = 256
S_DEV = 8
highest = lax.Precision.HIGHEST


def passed_along(block, axis, distance):
    devices = range(lax.axis_size(axis))
    route = [((i - distance) % len(devices), i) for i in devices]
    return lax.ppermute(block, axis, route)


def spline_weights(fraction):
    remain = 1.0 - fraction
    square = fraction * fraction
    cubic_term = square * fraction
    values = [
        remain * remain * remain / 6.0,
        (3.0 * cubic_term - 6.0 * square + 4.0) / 6.0,
        (-3.0 * cubic_term + 3.0 * square + 3.0 * fraction + 1.0) / 6.0,
        cubic_term / 6.0,
    ]
    slopes = [
        -0.5 * remain * remain,
        0.5 * (3.0 * square - 4.0 * fraction),
        0.5 * (-3.0 * square + 2.0 * fraction + 1.0),
        0.5 * square,
    ]
    return (values, slopes)


def place_weights(weights, local, width, period):
    columns = lax.broadcasted_iota(jnp.int32, (local.shape[0], width), 1)
    result = jnp.zeros((local.shape[0], width), jnp.float32)
    for offset in range(4):
        target = (local + offset) % period
        result = result + jnp.where(columns == target[:, None], weights[offset][:, None], 0.0)
    return result


def dft_tables(length):
    counter = lax.iota(jnp.int32, length)
    product = counter[:, None] * counter[None, :] % length
    angle = 2.0 * math.pi / length * product.astype(jnp.float32)
    return (jnp.cos(angle), jnp.sin(angle))


def rotate_pair(real_part, imag_part, pattern, cosine, sine, direction):
    real_cos = jnp.einsum(pattern, real_part, cosine, precision=highest)
    real_sin = jnp.einsum(pattern, real_part, sine, precision=highest)
    imag_cos = jnp.einsum(pattern, imag_part, cosine, precision=highest)
    imag_sin = jnp.einsum(pattern, imag_part, sine, precision=highest)
    return (real_cos - direction * imag_sin, imag_cos + direction * real_sin)


def body(charges, structure_id, live_count, cell_index, fraction, influence):
    atom_total = charges.shape[0]
    row_count = lax.axis_size("row")
    col_count = lax.axis_size("col")
    mesh_x = CX * row_count
    mesh_y = CY * col_count
    structures = S_DEV * row_count * col_count
    local_x = cell_index[0] - lax.axis_index("row") * CX
    local_y = cell_index[1] - lax.axis_index("col") * CY
    live = (lax.iota(jnp.int32, atom_total) < live_count[0]).astype(jnp.float32)
    wx_val, wx_slope = spline_weights(fraction[0])
    wy_val, wy_slope = spline_weights(fraction[1])
    wz_val, wz_slope = spline_weights(fraction[2])
    big_period = 4 * (CX + CY + 8)
    x_rows = place_weights(wx_val, local_x, CX + 3, big_period)
    x_slope_rows = place_weights(wx_slope, local_x, CX + 3, big_period)
    y_rows = place_weights(wy_val, local_y, CY + 3, big_period)
    y_slope_rows = place_weights(wy_slope, local_y, CY + 3, big_period)
    z_rows = place_weights(wz_val, cell_index[2], NZ, NZ)
    z_slope_rows = place_weights(wz_slope, cell_index[2], NZ, NZ)
    plane = (y_rows[:, :, None] * x_rows[:, None, :]).reshape(atom_total, -1)
    charge_sums = jax.ops.segment_sum(charges * live, structure_id, num_segments=structures)
    live_sums = jax.ops.segment_sum(live, structure_id, num_segments=structures)
    totals, counts = lax.psum((charge_sums, live_sums), ("row", "col"))
    neutral = (charges - jnp.take(totals / counts, structure_id)) * live
    spread_grid = lax.dot_general(
        plane,
        neutral[:, None] * z_rows,
        (((0,), (0,)), ((), ())),
        precision=highest,
        preferred_element_type=jnp.float32,
    )
    extended = spread_grid.reshape(CY + 3, CX + 3, NZ)
    spill_x = passed_along(extended[:, CX:, :], "row", 1)
    extended = extended[:, :CX, :].at[:, :3, :].add(spill_x)
    spill_y = passed_along(extended[CY:], "col", 1)
    density = extended[:CY].at[:3].add(spill_y)
    cos_z, sin_z = dft_tables(NZ)
    cos_y, sin_y = dft_tables(mesh_y)
    cos_x, sin_x = dft_tables(mesh_x)
    real_z = jnp.einsum("yxz,zk->kxy", density, cos_z, precision=highest)
    imag_z = -jnp.einsum("yxz,zk->kxy", density, sin_z, precision=highest)
    columns = lax.all_to_all(
        jnp.stack([real_z, imag_z]), "col", split_axis=1, concat_axis=3, tiled=True
    )
    real_y, imag_y = rotate_pair(columns[0], columns[1], "zxy,yk->zkx", cos_y, sin_y, -1.0)
    rows = lax.all_to_all(
        jnp.stack([real_y, imag_y]), "row", split_axis=2, concat_axis=3, tiled=True
    )
    real_x, imag_x = rotate_pair(rows[0], rows[1], "zyx,xk->zyk", cos_x, sin_x, -1.0)
    scale = influence / float(mesh_x * mesh_y * NZ)
    real_x = real_x * scale
    imag_x = imag_x * scale
    back_x, back_x_imag = rotate_pair(real_x, imag_x, "zyk,kx->zyx", cos_x, sin_x, 1.0)
    returned = lax.all_to_all(
        jnp.stack([back_x, back_x_imag]), "row", split_axis=3, concat_axis=2, tiled=True
    )
    back_y, back_y_imag = rotate_pair(returned[0], returned[1], "zkx,ky->zxy", cos_y, sin_y, 1.0)
    whole_z = lax.all_to_all(
        jnp.stack([back_y, back_y_imag]), "col", split_axis=3, concat_axis=1, tiled=True
    )
    potential = jnp.einsum("kxy,kz->yxz", whole_z[0], cos_z, precision=highest) - jnp.einsum(
        "kxy,kz->yxz", whole_z[1], sin_z, precision=highest
    )
    upper_x = passed_along(potential[:, :3, :], "row", -1)
    widened = jnp.concatenate([potential, upper_x], axis=1)
    upper_y = passed_along(widened[:3], "col", -1)
    widened = jnp.concatenate([widened, upper_y], axis=0).reshape(-1, NZ)
    sampled = lax.dot_general(
        jnp.concatenate([z_rows, z_slope_rows], axis=0),
        widened,
        (((1,), (1,)), ((), ())),
        precision=highest,
        preferred_element_type=jnp.float32,
    )
    sample_val = sampled[:atom_total]
    sample_slope = sampled[atom_total:]
    plane_dx = (y_rows[:, :, None] * x_slope_rows[:, None, :]).reshape(atom_total, -1)
    plane_dy = (y_slope_rows[:, :, None] * x_rows[:, None, :]).reshape(atom_total, -1)
    value = jnp.sum(plane * sample_val, axis=1)
    grad_x = jnp.sum(plane_dx * sample_val, axis=1)
    grad_y = jnp.sum(plane_dy * sample_val, axis=1)
    grad_z = jnp.sum(plane * sample_slope, axis=1)
    atom_energy = 0.5 * neutral * value
    forces = -neutral[None, :] * jnp.stack([grad_x, grad_y, grad_z])
    return (forces, atom_energy)


def solution(mesh):
    placed = (
        P(("row", "col")),
        P(("row", "col")),
        P(("row", "col")),
        P(None, ("row", "col")),
        P(None, ("row", "col")),
        P("col", "row", None),
    )
    return jax.shard_map(
        body,
        mesh=mesh,
        in_specs=placed,
        out_specs=(P(None, ("row", "col")), P(("row", "col"))),
        check_vma=False,
    )
```

profile of v0, /device:TPU:3, one launch (start us, length us, event | category | flops | bytes accessed | tf_op | source)
XLA Modules:
  0.0 171.7 jit_solution(16986416854421868476)
XLA Ops:
  1.3 0.7 fusion.132
  2.0 0.7 fusion.131
  2.7 7.7 %scatter_custom_fusion = f32[256]{0:T(256)S(1)} fusion(s32[1024]{0:T(1024)} %param.11, f32[1024]{0:T(1024)S(1)} %fusion.131, f32[]{:T(128)} %constant.237.clone.1), kind=kCustom, calls=%fused_computation.243 | custom fusion | flops 1024 | bytes 1536 | tf_op jit(solution)/shard_map/scatter-add | solution.py:84
  10.4 7.7 %scatter_custom_fusion.1 = f32[256]{0:T(256)S(1)} fusion(s32[1024]{0:T(1024)} %param.11, f32[1024]{0:T(1024)S(1)} %fusion.130, f32[]{:T(128)} %constant.237.clone.1), kind=kCustom, calls=%fused_computation.241 | custom fusion | flops 1024 | bytes 1536 | tf_op jit(solution)/shard_map/scatter-add | solution.py:85
  18.2 0.8 fusion.226
  19.1 0.8 fusion.227
  20.1 1.9 %broadcast_multiply_fusion.2 = (f32[1024,19,11]{0,2,1:T(8,128)}, f32[1024,19,11]{0,2,1:T(8,128)S(1)}, f32[1024,19,11]{0,2,1:T(8,128)}) fusion(f32[1024,11]{0,1:T(8,128)S(1)} %get-tuple-element.45, f32[1024,19]{0,1:T(8,128)S(1)} %get-tuple-element.48, f32[1024,11]{0,1:T(8,128)S(1)} %get-tuple-element.46, f32[1024,19]{0,1:T(8,128)S(1)} %get-tuple-element.47), kind=kLoop, calls=%fused_computation.46 | loop fusion | flops 642048 | bytes 2813952 | tf_op jit(solution)/shard_map/mul | solution.py:140
  22.3 39.6 %all-reduce = (f32[256]{0:T(256)S(1)}, f32[256]{0:T(256)S(1)}) all-reduce(f32[256]{0:T(256)S(1)} %scatter_custom_fusion, f32[256]{0:T(256)S(1)} %scatter_custom_fusion.1), channel_id=1, replica_groups=mesh['row'=8,'col'=4] {'row','col'}, use_global_device_ids=true, to_apply=%region_1.2 | all-reduce | flops 512 | bytes 4096 | tf_op jit(solution)/shard_map/psum | solution.py:86
  61.9 6.8 %gather_fusion = f32[1024]{0:T(1024)S(1)} fusion(f32[256]{0:T(256)S(1)} %div.45, s32[1024]{0:T(1024)S(1)} %fusion.132), kind=kCustom, calls=%fused_computation | custom fusion | bytes 12288 | tf_op jit(solution)/shard_map/jit(_take)/gather | solution.py:87
  68.8 0.6 multiply_multiply_fusion.2
  69.5 2.2 %fusion.17 = f32[19,11,256]{2,1,0:T(8,128)S(1)} fusion(f32[19,11,1024]{2,1,0:T(8,128)S(1)} %dot_general.71, f32[1024]{0:T(1024)S(1)} %get-tuple-element.94, f32[1024]{0:T(1024)S(1)} %get-tuple-element.79, s32[1024]{0:T(1024)S(1)} %get-tuple-element.84, f32[1024]{0:T(1024)S(1)} %get-tuple-element.78, s32[1024]{0:T(1024)S(1)} %get-tuple-element.83, ...), kind=kOutput, calls=%fused_computation.30 | convolution fusion | flops 660602880 | bytes 1106944 | tf_op jit(solution)/shard_map/dot_general | solution.py:88
  71.7 1.4 collective-permute-start
  73.1 1.9 %collective-permute-done = f32[19,3,256]{2,1,0:T(4,128)S(1)} collective-permute-done((f32[19,3,256]{2,1,0:T(4,128)S(1)}, f32[19,3,256]{2,1,0:T(4,128)S(1)}, u32[]{:S(2)}, u32[]{:S(2)}) %collective-permute-start) | collective-permute-done | bytes 58400 | tf_op jit(solution)/shard_map/ppermute | solution.py:17
  75.3 3.8 %collective-permute-start.1 = (f32[3,8,256]{2,1,0:T(8,128)S(1)}, f32[3,8,256]{2,1,0:T(8,128)S(1)}, u32[]{:S(2)}, u32[]{:S(2)}) collective-permute-start(f32[3,8,256]{2,1,0:T(8,128)S(1)} %slice.156), channel_id=1, source_target_pairs={{3,0},{0,1},{1,2},{2,3},{7,4},{4,5},{5,6},{6,7},{11,8},{8,9},{9,10... | collective-permute-start | bytes 73736 | tf_op jit(solution)/shard_map/ppermute | solution.py:17
  79.1 0.9 collective-permute-done.1
  80.1 1.3 fusion.16
  81.4 1.3 convolution_bitcast_fusion
  82.7 1.3 copy.81
  84.0 0.7 reshape.1016
  84.8 9.5 %all_to_all.60 = f32[4,1,16384]{2,1,0:T(1,128)S(1)} all-to-all(f32[4,1,16384]{2,1,0:T(1,128)S(1)} %reshape.1016), channel_id=1, replica_groups=mesh['row'=8,'col'=4] {'col'}, dimensions={0} | all-to-all | bytes 524288 | tf_op jit(solution)/shard_map/all_to_all | solution.py:105
  94.2 0.6 broadcast.1325
  94.8 1.3 reduce.4
  96.1 0.7 reshape.1017
  96.8 1.1 copy.128
  100.9 12.2 %all_to_all.61 = f32[8,1,8192]{2,1,0:T(1,128)S(1)} all-to-all(f32[8,1,8192]{2,1,0:T(1,128)S(1)} %reshape.1018), channel_id=1, replica_groups=mesh['row'=8,'col'=4] {'row'}, dimensions={0} | all-to-all | bytes 524288 | tf_op jit(solution)/shard_map/all_to_all | solution.py:109
  113.2 1.2 reduce.5
  114.7 0.6 fusion.29
  115.4 0.6 fusion.25
  116.0 0.6 fusion.11
  116.7 0.6 fusion.9
  120.0 11.0 %all_to_all.62 = f32[8,1,8192]{2,1,0:T(1,128)S(1)} all-to-all(f32[8,1,8192]{2,1,0:T(1,128)S(1)} %reshape.1020), channel_id=1, replica_groups=mesh['row'=8,'col'=4] {'row'}, dimensions={0} | all-to-all | bytes 524288 | tf_op jit(solution)/shard_map/all_to_all | solution.py:117
  131.0 1.2 reduce.6
  135.7 11.2 %all_to_all.63 = f32[4,1,16384]{2,1,0:T(1,128)S(1)} all-to-all(f32[4,1,16384]{2,1,0:T(1,128)S(1)} %reshape.1022), channel_id=1, replica_groups=mesh['row'=8,'col'=4] {'col'}, dimensions={0} | all-to-all | bytes 524288 | tf_op jit(solution)/shard_map/all_to_all | solution.py:121
  146.9 1.3 reduce.7
  149.1 1.3 fusion.45
  150.8 1.3 fusion.42
  152.5 3.6 %collective-permute-done.2 = f32[16,3,256]{2,0,1:T(8,128)S(1)} collective-permute-done((f32[16,3,256]{2,0,1:T(8,128)S(1)}, f32[16,3,256]{2,0,1:T(8,128)S(1)}, u32[]{:S(2)}, u32[]{:S(2)}) %collective-permute-start.2) | collective-permute-done | bytes 49184 | tf_op jit(solution)/shard_map/ppermute | solution.py:17
  156.0 0.6 pad_maximum_fusion.5
  156.7 2.2 %collective-permute-start.3 = (f32[3,11,256]{2,0,1:T(4,128)}, f32[3,11,256]{2,0,1:T(4,128)}, u32[]{:S(2)}, u32[]{:S(2)}) collective-permute-start(f32[3,11,256]{2,0,1:T(4,128)} %pad_maximum_fusion.5), channel_id=1, source_target_pairs={{1,0},{2,1},{3,2},{0,3},{5,4},{6,5},{7,6},{4,7},{9,8},{10,9},{11,1... | collective-permute-start | bytes 101384 | tf_op jit(solution)/shard_map/ppermute | solution.py:17
  158.9 3.1 %select_add_fusion.1 = (f32[1024,256]{1,0:T(8,128)}, f32[1024,256]{1,0:T(8,128)}) fusion(f32[1024]{0:T(1024)S(1)} %copy-done.16, s32[1024]{0:T(1024)S(1)} %copy-done.26, f32[1024]{0:T(1024)S(1)} %copy-done.14, s32[1024]{0:T(1024)S(1)} %copy-done.24, f32[1024]{0:T(1024)S(1)} %copy-done.18, s32[1024]{0:T(1024)S(1)} %copy-done.22, f32[1024]{0:T(1024)S(1)} %copy-done.11, ...), kind=kLoop, calls=%fused_computation.34 | loop fusion | flops 4718592 | bytes 2146304 | tf_op jit(solution)/shard_map/add | solution.py:44
  162.0 1.0 mul.759
  163.1 0.6 copy-done
  163.7 1.0 mul.815
  164.7 0.9 pad_maximum_fusion.3
  165.7 0.7 reshape.969
  166.4 3.3 %fusion = f32[2048,209]{0,1:T(8,128)S(1)} fusion(f32[209,256]{1,0:T(8,128)} %reshape.969, f32[1024,256]{1,0:T(8,128)S(1)} %copy-done.3, f32[1024,256]{1,0:T(8,128)S(1)} %copy-done.2), kind=kOutput, calls=%fused_computation.3 | convolution fusion | flops 1315438592 | bytes 4023296 | tf_op jit(solution)/shard_map/dot_general | solution.py:131
  170.4 0.6 multiply_multiply_fusion.21
  171.0 0.6 maximum_multiply_fusion
  (129 shorter events, 12.3 us)
Async XLA Ops:
  19.1 50.4 %copy-start.19 = (s32[1024]{0:T(1024)}, s32[1024]{0:T(1024)S(1)}, u32[]{:S(2)}) copy-start(s32[1024]{0:T(1024)S(1)} %get-tuple-element.81) | copy-start | bytes 12292
  19.1 50.4 %copy-start.21 = (s32[1024]{0:T(1024)}, s32[1024]{0:T(1024)S(1)}, u32[]{:S(2)}) copy-start(s32[1024]{0:T(1024)S(1)} %get-tuple-element.82) | copy-start | bytes 12292
  19.1 50.4 %copy-start.23 = (s32[1024]{0:T(1024)}, s32[1024]{0:T(1024)S(1)}, u32[]{:S(2)}) copy-start(s32[1024]{0:T(1024)S(1)} %get-tuple-element.83) | copy-start | bytes 12292
  19.1 50.4 %copy-start.25 = (s32[1024]{0:T(1024)}, s32[1024]{0:T(1024)S(1)}, u32[]{:S(2)}) copy-start(s32[1024]{0:T(1024)S(1)} %get-tuple-element.84) | copy-start | bytes 12292
  61.9 6.8 %copy-start.29 = (f32[1024]{0:T(1024)S(1)}, f32[1024]{0:T(1024)}, u32[]{:S(2)}) copy-start(f32[1024]{0:T(1024)} %param.10) | copy-start | bytes 12292
  61.9 6.9 %copy-start.30 = (s32[1024]{0:T(1024)S(1)}, s32[1024]{0:T(1024)}, u32[]{:S(2)}) copy-start(s32[1024]{0:T(1024)} %param.11) | copy-start | bytes 12292
  69.4 2.3 %copy-start.10 = (f32[1024]{0:T(1024)}, f32[1024]{0:T(1024)S(1)}, u32[]{:S(2)}) copy-start(f32[1024]{0:T(1024)S(1)} %get-tuple-element.76) | copy-start | bytes 12292
  69.4 2.3 %copy-start.13 = (f32[1024]{0:T(1024)}, f32[1024]{0:T(1024)S(1)}, u32[]{:S(2)}) copy-start(f32[1024]{0:T(1024)S(1)} %get-tuple-element.78) | copy-start | bytes 12292
  69.4 2.3 %copy-start.15 = (f32[1024]{0:T(1024)}, f32[1024]{0:T(1024)S(1)}, u32[]{:S(2)}) copy-start(f32[1024]{0:T(1024)S(1)} %get-tuple-element.79) | copy-start | bytes 12292
  69.4 2.3 %copy-start.17 = (f32[1024]{0:T(1024)}, f32[1024]{0:T(1024)S(1)}, u32[]{:S(2)}) copy-start(f32[1024]{0:T(1024)S(1)} %get-tuple-element.80) | copy-start | bytes 12292
  69.4 2.3 %copy-start.27 = (f32[1024]{0:T(1024)}, f32[1024]{0:T(1024)S(1)}, u32[]{:S(2)}) copy-start(f32[1024]{0:T(1024)S(1)} %get-tuple-element.94) | copy-start | bytes 12292
  71.7 3.3 %collective-permute-start = (f32[19,3,256]{2,1,0:T(4,128)S(1)}, f32[19,3,256]{2,1,0:T(4,128)S(1)}, u32[]{:S(2)}, u32[]{:S(2)}) collective-permute-start(f32[19,3,256]{2,1,0:T(4,128)S(1)} %slice.153), channel_id=1, source_target_pairs={{28,0},{0,4},{4,8},{8,12},{12,16},{16,20},{20,24},{24,28},{29,1},{... | collective-permute-start | bytes 175112 | tf_op jit(solution)/shard_map/ppermute | solution.py:17
  75.3 4.8 %collective-permute-start.1 = (f32[3,8,256]{2,1,0:T(8,128)S(1)}, f32[3,8,256]{2,1,0:T(8,128)S(1)}, u32[]{:S(2)}, u32[]{:S(2)}) collective-permute-start(f32[3,8,256]{2,1,0:T(8,128)S(1)} %slice.156), channel_id=1, source_target_pairs={{3,0},{0,1},{1,2},{2,3},{7,4},{4,5},{5,6},{6,7},{11,8},{8,9},{9,10... | collective-permute-start | bytes 73736 | tf_op jit(solution)/shard_map/ppermute | solution.py:17
  114.7 1.3 copy-start.6
  150.4 8.5 %copy-start.7 = (f32[1024]{0:T(1024)S(1)}, f32[1024]{0:T(1024)}, u32[]{:S(2)}) copy-start(f32[1024]{0:T(1024)} %get-tuple-element.73) | copy-start | bytes 12292
  150.4 8.5 %copy-start.8 = (f32[1024]{0:T(1024)S(1)}, f32[1024]{0:T(1024)}, u32[]{:S(2)}) copy-start(f32[1024]{0:T(1024)} %get-tuple-element.74) | copy-start | bytes 12292
  150.4 8.5 %copy-start.9 = (f32[1024]{0:T(1024)S(1)}, f32[1024]{0:T(1024)}, u32[]{:S(2)}) copy-start(f32[1024]{0:T(1024)} %get-tuple-element.75) | copy-start | bytes 12292
  150.4 8.5 %copy-start.11 = (f32[1024]{0:T(1024)S(1)}, f32[1024]{0:T(1024)}, u32[]{:S(2)}) copy-start(f32[1024]{0:T(1024)} %copy-done.10) | copy-start | bytes 12292
  150.4 8.5 %copy-start.12 = (f32[1024]{0:T(1024)S(1)}, f32[1024]{0:T(1024)}, u32[]{:S(2)}) copy-start(f32[1024]{0:T(1024)} %get-tuple-element.77) | copy-start | bytes 12292
  150.4 8.5 %copy-start.14 = (f32[1024]{0:T(1024)S(1)}, f32[1024]{0:T(1024)}, u32[]{:S(2)}) copy-start(f32[1024]{0:T(1024)} %copy-done.13) | copy-start | bytes 12292
  150.4 8.5 %copy-start.16 = (f32[1024]{0:T(1024)S(1)}, f32[1024]{0:T(1024)}, u32[]{:S(2)}) copy-start(f32[1024]{0:T(1024)} %copy-done.15) | copy-start | bytes 12292
  150.4 8.5 %copy-start.18 = (f32[1024]{0:T(1024)S(1)}, f32[1024]{0:T(1024)}, u32[]{:S(2)}) copy-start(f32[1024]{0:T(1024)} %copy-done.17) | copy-start | bytes 12292
  150.4 8.5 %copy-start.20 = (s32[1024]{0:T(1024)S(1)}, s32[1024]{0:T(1024)}, u32[]{:S(2)}) copy-start(s32[1024]{0:T(1024)} %copy-done.19) | copy-start | bytes 12292
  150.5 8.5 %copy-start.22 = (s32[1024]{0:T(1024)S(1)}, s32[1024]{0:T(1024)}, u32[]{:S(2)}) copy-start(s32[1024]{0:T(1024)} %copy-done.21) | copy-start | bytes 12292
  150.5 8.5 %copy-start.24 = (s32[1024]{0:T(1024)S(1)}, s32[1024]{0:T(1024)}, u32[]{:S(2)}) copy-start(s32[1024]{0:T(1024)} %copy-done.23) | copy-start | bytes 12292
  150.5 8.5 %copy-start.26 = (s32[1024]{0:T(1024)S(1)}, s32[1024]{0:T(1024)}, u32[]{:S(2)}) copy-start(s32[1024]{0:T(1024)} %copy-done.25) | copy-start | bytes 12292
  152.1 9.9 %copy-start.1 = (f32[1024,19,11]{0,2,1:T(8,128)S(1)}, f32[1024,19,11]{0,2,1:T(8,128)}, u32[]{:S(2)}) copy-start(f32[1024,19,11]{0,2,1:T(8,128)} %get-tuple-element.42) | copy-start | bytes 2568196
  152.1 3.9 %collective-permute-start.2 = (f32[16,3,256]{2,0,1:T(8,128)S(1)}, f32[16,3,256]{2,0,1:T(8,128)S(1)}, u32[]{:S(2)}, u32[]{:S(2)}) collective-permute-start(f32[16,3,256]{2,0,1:T(8,128)S(1)} %slice.165), channel_id=1, source_target_pairs={{4,0},{8,4},{12,8},{16,12},{20,16},{24,20},{28,24},{0,28},{5,1},{9... | collective-permute-start | bytes 147464 | tf_op jit(solution)/shard_map/ppermute | solution.py:17
  156.7 8.0 %collective-permute-start.3 = (f32[3,11,256]{2,0,1:T(4,128)}, f32[3,11,256]{2,0,1:T(4,128)}, u32[]{:S(2)}, u32[]{:S(2)}) collective-permute-start(f32[3,11,256]{2,0,1:T(4,128)} %pad_maximum_fusion.5), channel_id=1, source_target_pairs={{1,0},{2,1},{3,2},{0,3},{5,4},{6,5},{7,6},{4,7},{9,8},{10,9},{11,1... | collective-permute-start | bytes 101384 | tf_op jit(solution)/shard_map/ppermute | solution.py:17
  162.0 1.6 copy-start
  163.7 2.8 %copy-start.3 = (f32[1024,256]{1,0:T(8,128)S(1)}, f32[1024,256]{1,0:T(8,128)}, u32[]{:S(2)}) copy-start(f32[1024,256]{1,0:T(8,128)} %get-tuple-element.50) | copy-start | bytes 3145732
  164.7 1.7 %copy-start.2 = (f32[1024,256]{1,0:T(8,128)S(1)}, f32[1024,256]{1,0:T(8,128)}, u32[]{:S(2)}) copy-start(f32[1024,256]{1,0:T(8,128)} %get-tuple-element.49) | copy-start | bytes 3145732
  166.4 3.3 %copy-start.4 = (f32[1024,209]{0,1:T(8,128)S(1)}, f32[1024,209]{0,1:T(8,128)}, u32[]{:S(2)}) copy-start(f32[1024,209]{0,1:T(8,128)} %mul.759) | copy-start | bytes 2568196
  166.4 3.3 %copy-start.5 = (f32[1024,209]{0,1:T(8,128)S(1)}, f32[1024,209]{0,1:T(8,128)}, u32[]{:S(2)}) copy-start(f32[1024,209]{0,1:T(8,128)} %mul.815) | copy-start | bytes 2568196
  169.8 0.7 copy-start.28
  169.8 1.3 copy-start.31
where the time goes:
time: 172 us
  blocking collectives  83.5 us (49%)
  other arithmetic  32.2 us (19%)
  local copies, waits for them, and re-layouts  20.3 us (12%)
  matrix products  19.3 us (11%)
  starting transfers between devices  7.72 us (4%)
  waiting for transfers between devices  6.39 us (4%)
  between operations  2.24 us (1%)
    psum x1, blocking collectives, body(): totals, counts = lax.psum((charge_sums, live_sums), ('row', 'col'))  39.6 us
    all_to_all x1, blocking collectives, body(): lax.all_to_all(jnp.stack([real_y, imag_y]), 'row', split_axis=2, concat_a...  12.2 us
    all_to_all x1, blocking collectives, body(): lax.all_to_all(jnp.stack([back_y, back_y_imag]), 'col', split_axis=3, con...  11.2 us
    all_to_all x1, blocking collectives, body(): lax.all_to_all(jnp.stack([back_x, back_x_imag]), 'row', split_axis=3, con...  11 us
    all_to_all x1, blocking collectives, body(): lax.all_to_all(jnp.stack([real_z, imag_z]), 'col', split_axis=1, concat_a...  9.47 us
    scatter-add x1, other arithmetic, body(): live_sums = jax.ops.segment_sum(live, structure_id, num_segments=structures)  7.75 us
    scatter-add x1, other arithmetic, body(): jax.ops.segment_sum(charges * live, structure_id, num_segments=structures)  7.74 us
    ppermute x4, starting transfers between devices, passed_along(): return lax.ppermute(block, axis, route)  7.72 us
  transfers between devices with their start and end apart: 4, of which 3 were waited for; matrix products, arithmetic and copies ran while one was open for 3% of the time, Pallas kernels for 0%

commit v1 on v0

--- a/solution.py
+++ b/solution.py
@@ -83,7 +83,7 @@
     plane = (y_rows[:, :, None] * x_rows[:, None, :]).reshape(atom_total, -1)
     charge_sums = jax.ops.segment_sum(charges * live, structure_id, num_segments=structures)
     live_sums = jax.ops.segment_sum(live, structure_id, num_segments=structures)
-    totals, counts = lax.psum((charge_sums, live_sums), ("row", "col"))
+    totals, counts = lax.psum(lax.psum((charge_sums, live_sums), "col"), "row")
     neutral = (charges - jnp.take(totals / counts, structure_id)) * live
     spread_grid = lax.dot_general(
         plane,

time: 172 us -> 159 us (0.924)
  blocking collectives: 83.5 us -> 65.2 us
  starting transfers between devices: 7.72 us -> 11.4 us
    psum x1 -> x2, blocking collectives: 39.6 us -> 19.9 us  [body(): totals, counts = lax.psum(lax.psum((charge_sums, live_sums), 'col'), 'row')]
    ppermute x4, starting transfers between devices: 7.72 us -> 11.4 us  [passed_along(): return lax.ppermute(block, axis, route)]
where the time goes in v1:
time: 159 us; the launch traced here: 158 us
  blocking collectives  65.2 us (41%)
  other arithmetic  31.9 us (20%)
  local copies, waits for them, and re-layouts  20.2 us (13%)
  matrix products  19.3 us (12%)
  starting transfers between devices  11.4 us (7%)
  waiting for transfers between devices  8.06 us (5%)
  between operations  2.24 us (1%)
    psum x2, blocking collectives, body(): totals, counts = lax.psum(lax.psum((charge_sums, live_sums), 'col'), 'row')  19.9 us
    all_to_all x1, blocking collectives, body(): lax.all_to_all(jnp.stack([real_y, imag_y]), 'row', split_axis=2, concat_a...  13.6 us
    ppermute x4, starting transfers between devices, passed_along(): return lax.ppermute(block, axis, route)  11.4 us
    all_to_all x1, blocking collectives, body(): lax.all_to_all(jnp.stack([back_y, back_y_imag]), 'col', split_axis=3, con...  11.2 us
    all_to_all x1, blocking collectives, body(): lax.all_to_all(jnp.stack([back_x, back_x_imag]), 'row', split_axis=3, con...  11 us
    all_to_all x1, blocking collectives, body(): lax.all_to_all(jnp.stack([real_z, imag_z]), 'col', split_axis=1, concat_a...  9.58 us
    ppermute x4, waiting for transfers between devices, passed_along(): return lax.ppermute(block, axis, route)  8.06 us
    scatter-add x1, other arithmetic, body(): live_sums = jax.ops.segment_sum(live, structure_id, num_segments=structures)  7.75 us
  transfers between devices with their start and end apart: 4, of which 3 were waited for; matrix products, arithmetic and copies ran while one was open for 3% of the time, Pallas kernels for 0%

profile of v1, /device:TPU:3, one launch (start us, length us, event | category | flops | bytes accessed | tf_op | source)
XLA Modules:
  0.0 158.3 jit_solution(15726108056464002537)
XLA Ops:
  1.3 0.7 fusion.132
  2.0 0.7 fusion.131
  2.7 7.7 %scatter_custom_fusion = f32[256]{0:T(256)S(1)} fusion(s32[1024]{0:T(1024)} %param.11, f32[1024]{0:T(1024)S(1)} %fusion.131, f32[]{:T(128)} %constant.237.clone.1), kind=kCustom, calls=%fused_computation.243 | custom fusion | flops 1024 | bytes 1536 | tf_op jit(solution)/shard_map/scatter-add | solution.py:84
  10.4 7.7 %scatter_custom_fusion.1 = f32[256]{0:T(256)S(1)} fusion(s32[1024]{0:T(1024)} %param.11, f32[1024]{0:T(1024)S(1)} %fusion.130, f32[]{:T(128)} %constant.237.clone.1), kind=kCustom, calls=%fused_computation.241 | custom fusion | flops 1024 | bytes 1536 | tf_op jit(solution)/shard_map/scatter-add | solution.py:85
  18.2 0.8 fusion.226
  19.1 0.8 fusion.227
  20.1 1.9 %broadcast_multiply_fusion.2 = (f32[1024,19,11]{0,2,1:T(8,128)}, f32[1024,19,11]{0,2,1:T(8,128)S(1)}, f32[1024,19,11]{0,2,1:T(8,128)}) fusion(f32[1024,11]{0,1:T(8,128)S(1)} %get-tuple-element.47, f32[1024,19]{0,1:T(8,128)S(1)} %get-tuple-element.50, f32[1024,11]{0,1:T(8,128)S(1)} %get-tuple-element.48, f32[1024,19]{0,1:T(8,128)S(1)} %get-tuple-element.49), kind=kLoop, calls=%fused_computation.46 | loop fusion | flops 642048 | bytes 2813952 | tf_op jit(solution)/shard_map/mul | solution.py:140
  22.3 5.7 %all-reduce.1 = (f32[256]{0:T(256)S(1)}, f32[256]{0:T(256)S(1)}) all-reduce(f32[256]{0:T(256)S(1)} %scatter_custom_fusion, f32[256]{0:T(256)S(1)} %scatter_custom_fusion.1), channel_id=1, replica_groups=mesh['row'=8,'col'=4] {'col'}, use_global_device_ids=true, to_apply=%region_1.2 | all-reduce | flops 512 | bytes 4096 | tf_op jit(solution)/shard_map/psum | solution.py:86
  28.0 14.2 %all-reduce = (f32[256]{0:T(256)S(1)}, f32[256]{0:T(256)S(1)}) all-reduce(f32[256]{0:T(256)S(1)} %get-tuple-element.32, f32[256]{0:T(256)S(1)} %get-tuple-element.33), channel_id=1, replica_groups=mesh['row'=8,'col'=4] {'row'}, use_global_device_ids=true, to_apply=%region_2.3 | all-reduce | flops 512 | bytes 4096 | tf_op jit(solution)/shard_map/psum | solution.py:86
  42.2 6.8 %gather_fusion = f32[1024]{0:T(1024)S(1)} fusion(f32[256]{0:T(256)S(1)} %div.45, s32[1024]{0:T(1024)S(1)} %fusion.132), kind=kCustom, calls=%fused_computation | custom fusion | bytes 12288 | tf_op jit(solution)/shard_map/jit(_take)/gather | solution.py:87
  49.1 0.6 multiply_multiply_fusion.2
  49.8 2.2 %fusion.17 = f32[19,11,256]{2,1,0:T(8,128)S(1)} fusion(f32[19,11,1024]{2,1,0:T(8,128)S(1)} %dot_general.71, f32[1024]{0:T(1024)S(1)} %get-tuple-element.96, f32[1024]{0:T(1024)S(1)} %get-tuple-element.81, s32[1024]{0:T(1024)S(1)} %get-tuple-element.86, f32[1024]{0:T(1024)S(1)} %get-tuple-element.80, s32[1024]{0:T(1024)S(1)} %get-tuple-element.85, ...), kind=kOutput, calls=%fused_computation.30 | convolution fusion | flops 660602880 | bytes 1106944 | tf_op jit(solution)/shard_map/dot_general | solution.py:88
  52.1 2.2 %collective-permute-start = (f32[19,3,256]{2,1,0:T(4,128)S(1)}, f32[19,3,256]{2,1,0:T(4,128)S(1)}, u32[]{:S(2)}, u32[]{:S(2)}) collective-permute-start(f32[19,3,256]{2,1,0:T(4,128)S(1)} %slice.153), channel_id=1, source_target_pairs={{28,0},{0,4},{4,8},{8,12},{12,16},{16,20},{20,24},{24,28},{29,1},{... | collective-permute-start | bytes 175112 | tf_op jit(solution)/shard_map/ppermute | solution.py:17
  54.3 3.6 %collective-permute-done = f32[19,3,256]{2,1,0:T(4,128)S(1)} collective-permute-done((f32[19,3,256]{2,1,0:T(4,128)S(1)}, f32[19,3,256]{2,1,0:T(4,128)S(1)}, u32[]{:S(2)}, u32[]{:S(2)}) %collective-permute-start) | collective-permute-done | bytes 58400 | tf_op jit(solution)/shard_map/ppermute | solution.py:17
  58.1 6.7 %collective-permute-start.1 = (f32[3,8,256]{2,1,0:T(8,128)S(1)}, f32[3,8,256]{2,1,0:T(8,128)S(1)}, u32[]{:S(2)}, u32[]{:S(2)}) collective-permute-start(f32[3,8,256]{2,1,0:T(8,128)S(1)} %slice.156), channel_id=1, source_target_pairs={{3,0},{0,1},{1,2},{2,3},{7,4},{4,5},{5,6},{6,7},{11,8},{8,9},{9,10... | collective-permute-start | bytes 73736 | tf_op jit(solution)/shard_map/ppermute | solution.py:17
  64.8 0.9 collective-permute-done.1
  65.7 1.3 fusion.16
  67.0 1.3 convolution_bitcast_fusion
  68.4 1.3 copy.81
  69.6 0.7 reshape.1016
  70.4 9.6 %all_to_all.60 = f32[4,1,16384]{2,1,0:T(1,128)S(1)} all-to-all(f32[4,1,16384]{2,1,0:T(1,128)S(1)} %reshape.1016), channel_id=1, replica_groups=mesh['row'=8,'col'=4] {'col'}, dimensions={0} | all-to-all | bytes 524288 | tf_op jit(solution)/shard_map/all_to_all | solution.py:105
  80.5 1.3 reduce.4
  81.7 0.7 reshape.1017
  82.4 1.1 copy.128
  86.5 13.6 %all_to_all.61 = f32[8,1,8192]{2,1,0:T(1,128)S(1)} all-to-all(f32[8,1,8192]{2,1,0:T(1,128)S(1)} %reshape.1018), channel_id=1, replica_groups=mesh['row'=8,'col'=4] {'row'}, dimensions={0} | all-to-all | bytes 524288 | tf_op jit(solution)/shard_map/all_to_all | solution.py:109
  100.1 1.2 reduce.5
  101.6 0.6 fusion.29
  102.2 0.6 fusion.25
  102.9 0.6 fusion.11
  103.5 0.6 fusion.9
  106.8 11.0 %all_to_all.62 = f32[8,1,8192]{2,1,0:T(1,128)S(1)} all-to-all(f32[8,1,8192]{2,1,0:T(1,128)S(1)} %reshape.1020), channel_id=1, replica_groups=mesh['row'=8,'col'=4] {'row'}, dimensions={0} | all-to-all | bytes 524288 | tf_op jit(solution)/shard_map/all_to_all | solution.py:117
  117.8 1.2 reduce.6
  122.5 11.2 %all_to_all.63 = f32[4,1,16384]{2,1,0:T(1,128)S(1)} all-to-all(f32[4,1,16384]{2,1,0:T(1,128)S(1)} %reshape.1022), channel_id=1, replica_groups=mesh['row'=8,'col'=4] {'col'}, dimensions={0} | all-to-all | bytes 524288 | tf_op jit(solution)/shard_map/all_to_all | solution.py:121
  133.6 1.3 reduce.7
  135.7 1.3 fusion.45
  137.5 1.3 fusion.42
  139.1 3.6 %collective-permute-done.2 = f32[16,3,256]{2,0,1:T(8,128)S(1)} collective-permute-done((f32[16,3,256]{2,0,1:T(8,128)S(1)}, f32[16,3,256]{2,0,1:T(8,128)S(1)}, u32[]{:S(2)}, u32[]{:S(2)}) %collective-permute-start.2) | collective-permute-done | bytes 49184 | tf_op jit(solution)/shard_map/ppermute | solution.py:17
  142.7 0.6 pad_maximum_fusion.5
  143.3 2.2 %collective-permute-start.3 = (f32[3,11,256]{2,0,1:T(4,128)}, f32[3,11,256]{2,0,1:T(4,128)}, u32[]{:S(2)}, u32[]{:S(2)}) collective-permute-start(f32[3,11,256]{2,0,1:T(4,128)} %pad_maximum_fusion.5), channel_id=1, source_target_pairs={{1,0},{2,1},{3,2},{0,3},{5,4},{6,5},{7,6},{4,7},{9,8},{10,9},{11,1... | collective-permute-start | bytes 101384 | tf_op jit(solution)/shard_map/ppermute | solution.py:17
  145.6 3.1 %select_add_fusion.1 = (f32[1024,256]{1,0:T(8,128)}, f32[1024,256]{1,0:T(8,128)}) fusion(f32[1024]{0:T(1024)S(1)} %copy-done.16, s32[1024]{0:T(1024)S(1)} %copy-done.26, f32[1024]{0:T(1024)S(1)} %copy-done.14, s32[1024]{0:T(1024)S(1)} %copy-done.24, f32[1024]{0:T(1024)S(1)} %copy-done.18, s32[1024]{0:T(1024)S(1)} %copy-done.22, f32[1024]{0:T(1024)S(1)} %copy-done.11, ...), kind=kLoop, calls=%fused_computation.34 | loop fusion | flops 4718592 | bytes 2146304 | tf_op jit(solution)/shard_map/add | solution.py:44
  148.7 1.1 mul.759
  149.8 0.6 copy-done
  150.3 1.0 mul.815
  151.4 0.9 pad_maximum_fusion.3
  152.4 0.7 reshape.969
  153.1 3.3 %fusion = f32[2048,209]{0,1:T(8,128)S(1)} fusion(f32[209,256]{1,0:T(8,128)} %reshape.969, f32[1024,256]{1,0:T(8,128)S(1)} %copy-done.3, f32[1024,256]{1,0:T(8,128)S(1)} %copy-done.2), kind=kOutput, calls=%fused_computation.3 | convolution fusion | flops 1315438592 | bytes 4023296 | tf_op jit(solution)/shard_map/dot_general | solution.py:131
  157.1 0.6 multiply_multiply_fusion.21
  157.7 0.6 maximum_multiply_fusion
  (130 shorter events, 12.8 us)
Async XLA Ops:
  19.1 30.7 %copy-start.19 = (s32[1024]{0:T(1024)}, s32[1024]{0:T(1024)S(1)}, u32[]{:S(2)}) copy-start(s32[1024]{0:T(1024)S(1)} %get-tuple-element.83) | copy-start | bytes 12292
  19.1 30.7 %copy-start.21 = (s32[1024]{0:T(1024)}, s32[1024]{0:T(1024)S(1)}, u32[]{:S(2)}) copy-start(s32[1024]{0:T(1024)S(1)} %get-tuple-element.84) | copy-start | bytes 12292
  19.1 30.7 %copy-start.23 = (s32[1024]{0:T(1024)}, s32[1024]{0:T(1024)S(1)}, u32[]{:S(2)}) copy-start(s32[1024]{0:T(1024)S(1)} %get-tuple-element.85) | copy-start | bytes 12292
  19.1 30.7 %copy-start.25 = (s32[1024]{0:T(1024)}, s32[1024]{0:T(1024)S(1)}, u32[]{:S(2)}) copy-start(s32[1024]{0:T(1024)S(1)} %get-tuple-element.86) | copy-start | bytes 12292
  42.2 6.9 %copy-start.29 = (f32[1024]{0:T(1024)S(1)}, f32[1024]{0:T(1024)}, u32[]{:S(2)}) copy-start(f32[1024]{0:T(1024)} %param.10) | copy-start | bytes 12292
  42.2 6.9 %copy-start.30 = (s32[1024]{0:T(1024)S(1)}, s32[1024]{0:T(1024)}, u32[]{:S(2)}) copy-start(s32[1024]{0:T(1024)} %param.11) | copy-start | bytes 12292
  49.7 2.3 %copy-start.10 = (f32[1024]{0:T(1024)}, f32[1024]{0:T(1024)S(1)}, u32[]{:S(2)}) copy-start(f32[1024]{0:T(1024)S(1)} %get-tuple-element.78) | copy-start | bytes 12292
  49.7 2.3 %copy-start.13 = (f32[1024]{0:T(1024)}, f32[1024]{0:T(1024)S(1)}, u32[]{:S(2)}) copy-start(f32[1024]{0:T(1024)S(1)} %get-tuple-element.80) | copy-start | bytes 12292
  49.7 2.3 %copy-start.15 = (f32[1024]{0:T(1024)}, f32[1024]{0:T(1024)S(1)}, u32[]{:S(2)}) copy-start(f32[1024]{0:T(1024)S(1)} %get-tuple-element.81) | copy-start | bytes 12292
  49.7 2.3 %copy-start.17 = (f32[1024]{0:T(1024)}, f32[1024]{0:T(1024)S(1)}, u32[]{:S(2)}) copy-start(f32[1024]{0:T(1024)S(1)} %get-tuple-element.82) | copy-start | bytes 12292
  49.7 2.3 %copy-start.27 = (f32[1024]{0:T(1024)}, f32[1024]{0:T(1024)S(1)}, u32[]{:S(2)}) copy-start(f32[1024]{0:T(1024)S(1)} %get-tuple-element.96) | copy-start | bytes 12292
  52.1 5.8 %collective-permute-start = (f32[19,3,256]{2,1,0:T(4,128)S(1)}, f32[19,3,256]{2,1,0:T(4,128)S(1)}, u32[]{:S(2)}, u32[]{:S(2)}) collective-permute-start(f32[19,3,256]{2,1,0:T(4,128)S(1)} %slice.153), channel_id=1, source_target_pairs={{28,0},{0,4},{4,8},{8,12},{12,16},{16,20},{20,24},{24,28},{29,1},{... | collective-permute-start | bytes 175112 | tf_op jit(solution)/shard_map/ppermute | solution.py:17
  58.1 7.6 %collective-permute-start.1 = (f32[3,8,256]{2,1,0:T(8,128)S(1)}, f32[3,8,256]{2,1,0:T(8,128)S(1)}, u32[]{:S(2)}, u32[]{:S(2)}) collective-permute-start(f32[3,8,256]{2,1,0:T(8,128)S(1)} %slice.156), channel_id=1, source_target_pairs={{3,0},{0,1},{1,2},{2,3},{7,4},{4,5},{5,6},{6,7},{11,8},{8,9},{9,10... | collective-permute-start | bytes 73736 | tf_op jit(solution)/shard_map/ppermute | solution.py:17
  101.5 1.3 copy-start.6
  137.0 8.5 %copy-start.7 = (f32[1024]{0:T(1024)S(1)}, f32[1024]{0:T(1024)}, u32[]{:S(2)}) copy-start(f32[1024]{0:T(1024)} %get-tuple-element.75) | copy-start | bytes 12292
  137.0 8.5 %copy-start.8 = (f32[1024]{0:T(1024)S(1)}, f32[1024]{0:T(1024)}, u32[]{:S(2)}) copy-start(f32[1024]{0:T(1024)} %get-tuple-element.76) | copy-start | bytes 12292
  137.1 8.5 %copy-start.9 = (f32[1024]{0:T(1024)S(1)}, f32[1024]{0:T(1024)}, u32[]{:S(2)}) copy-start(f32[1024]{0:T(1024)} %get-tuple-element.77) | copy-start | bytes 12292
  137.1 8.5 %copy-start.11 = (f32[1024]{0:T(1024)S(1)}, f32[1024]{0:T(1024)}, u32[]{:S(2)}) copy-start(f32[1024]{0:T(1024)} %copy-done.10) | copy-start | bytes 12292
  137.1 8.5 %copy-start.12 = (f32[1024]{0:T(1024)S(1)}, f32[1024]{0:T(1024)}, u32[]{:S(2)}) copy-start(f32[1024]{0:T(1024)} %get-tuple-element.79) | copy-start | bytes 12292
  137.1 8.5 %copy-start.14 = (f32[1024]{0:T(1024)S(1)}, f32[1024]{0:T(1024)}, u32[]{:S(2)}) copy-start(f32[1024]{0:T(1024)} %copy-done.13) | copy-start | bytes 12292
  137.1 8.5 %copy-start.16 = (f32[1024]{0:T(1024)S(1)}, f32[1024]{0:T(1024)}, u32[]{:S(2)}) copy-start(f32[1024]{0:T(1024)} %copy-done.15) | copy-start | bytes 12292
  137.1 8.5 %copy-start.18 = (f32[1024]{0:T(1024)S(1)}, f32[1024]{0:T(1024)}, u32[]{:S(2)}) copy-start(f32[1024]{0:T(1024)} %copy-done.17) | copy-start | bytes 12292
  137.1 8.5 %copy-start.20 = (s32[1024]{0:T(1024)S(1)}, s32[1024]{0:T(1024)}, u32[]{:S(2)}) copy-start(s32[1024]{0:T(1024)} %copy-done.19) | copy-start | bytes 12292
  137.1 8.5 %copy-start.22 = (s32[1024]{0:T(1024)S(1)}, s32[1024]{0:T(1024)}, u32[]{:S(2)}) copy-start(s32[1024]{0:T(1024)} %copy-done.21) | copy-start | bytes 12292
  137.1 8.5 %copy-start.24 = (s32[1024]{0:T(1024)S(1)}, s32[1024]{0:T(1024)}, u32[]{:S(2)}) copy-start(s32[1024]{0:T(1024)} %copy-done.23) | copy-start | bytes 12292
  137.1 8.5 %copy-start.26 = (s32[1024]{0:T(1024)S(1)}, s32[1024]{0:T(1024)}, u32[]{:S(2)}) copy-start(s32[1024]{0:T(1024)} %copy-done.25) | copy-start | bytes 12292
  138.8 10.0 %copy-start.1 = (f32[1024,19,11]{0,2,1:T(8,128)S(1)}, f32[1024,19,11]{0,2,1:T(8,128)}, u32[]{:S(2)}) copy-start(f32[1024,19,11]{0,2,1:T(8,128)} %get-tuple-element.44) | copy-start | bytes 2568196
  138.8 3.9 %collective-permute-start.2 = (f32[16,3,256]{2,0,1:T(8,128)S(1)}, f32[16,3,256]{2,0,1:T(8,128)S(1)}, u32[]{:S(2)}, u32[]{:S(2)}) collective-permute-start(f32[16,3,256]{2,0,1:T(8,128)S(1)} %slice.165), channel_id=1, source_target_pairs={{4,0},{8,4},{12,8},{16,12},{20,16},{24,20},{28,24},{0,28},{5,1},{9... | collective-permute-start | bytes 147464 | tf_op jit(solution)/shard_map/ppermute | solution.py:17
  143.3 8.1 %collective-permute-start.3 = (f32[3,11,256]{2,0,1:T(4,128)}, f32[3,11,256]{2,0,1:T(4,128)}, u32[]{:S(2)}, u32[]{:S(2)}) collective-permute-start(f32[3,11,256]{2,0,1:T(4,128)} %pad_maximum_fusion.5), channel_id=1, source_target_pairs={{1,0},{2,1},{3,2},{0,3},{5,4},{6,5},{7,6},{4,7},{9,8},{10,9},{11,1... | collective-permute-start | bytes 101384 | tf_op jit(solution)/shard_map/ppermute | solution.py:17
  148.7 1.6 %copy-start = (f32[1024,19,11]{0,2,1:T(8,128)S(1)}, f32[1024,19,11]{0,2,1:T(8,128)}, u32[]{:S(2)}) copy-start(f32[1024,19,11]{0,2,1:T(8,128)} %get-tuple-element.46) | copy-start | bytes 2568196
  150.3 2.8 %copy-start.3 = (f32[1024,256]{1,0:T(8,128)S(1)}, f32[1024,256]{1,0:T(8,128)}, u32[]{:S(2)}) copy-start(f32[1024,256]{1,0:T(8,128)} %get-tuple-element.52) | copy-start | bytes 3145732
  151.4 1.7 %copy-start.2 = (f32[1024,256]{1,0:T(8,128)S(1)}, f32[1024,256]{1,0:T(8,128)}, u32[]{:S(2)}) copy-start(f32[1024,256]{1,0:T(8,128)} %get-tuple-element.51) | copy-start | bytes 3145732
  153.1 3.3 %copy-start.4 = (f32[1024,209]{0,1:T(8,128)S(1)}, f32[1024,209]{0,1:T(8,128)}, u32[]{:S(2)}) copy-start(f32[1024,209]{0,1:T(8,128)} %mul.759) | copy-start | bytes 2568196
  153.1 3.3 %copy-start.5 = (f32[1024,209]{0,1:T(8,128)S(1)}, f32[1024,209]{0,1:T(8,128)}, u32[]{:S(2)}) copy-start(f32[1024,209]{0,1:T(8,128)} %mul.815) | copy-start | bytes 2568196
  156.5 0.7 copy-start.28
  156.5 1.3 copy-start.31
